TPU v7x, 512 devices: a whole 4x4x16 slice. The times are simulated.
512 devices in a mesh: tm: 8 (over x, core), rows: 64 (over z, y).
Axes of the slice: x: 4, y: 4, z: 16, core: 2. Of those that a mesh axis runs over, the one named last changes fastest.
Arguments:
- features: bfloat16 [16, 128, 384, 128], P('tm', 'rows'), may hold values from -6 to 6
- conv_in: bfloat16 [3, 3, 3, 128, 128], replicated, may hold values from -0.109375 to 0.109375
- bias_in: float32 [128], replicated, may hold values from -3 to 3
- down_proj: bfloat16 [2, 2, 128, 256], replicated, may hold values from -0.25 to 0.25
- bias_down: float32 [256], replicated, may hold values from -3 to 3
- spatial_w: bfloat16 [3, 3, 256, 256], replicated, may hold values from -0.125 to 0.125
- temporal_w: bfloat16 [3, 256, 256], replicated, may hold values from -0.21875 to 0.21875
- bias_mid: float32 [256], replicated, may hold values from -3 to 3
- norm_gain: float32 [256], replicated, may hold values from 0.1 to 1.9
- latent_proj: bfloat16 [256, 16], replicated, may hold values from -0.375 to 0.375
Outputs:
- latents: float32 [16, 192, 16, 64], P('tm', 'rows')
All inputs are finite; a program needn't handle non-finite values.
Results may differ from a plain program's by a relative error of at most 0.013.
Values may be sent and summed in bfloat16 or wider, within the bound.
A program may use at most 64 MiB of HBM per device.

v0:
```python
import jax
import jax.numpy as jnp
from jax import lax
from jax.sharding import PartitionSpec as P


def shifted(block, axis, distance):
    devices = range(lax.axis_size(axis))
    route = [(i - distance, i) for i in devices if i - distance in devices]
    return lax.ppermute(block, axis, route)


def with_halo(value, sides, width):
    for axis, dim in sides:
        peers, length = (lax.axis_size(axis), value.shape[dim])
        up = [(i, (i + 1) % peers) for i in range(peers - 1)]
        down = [(j, i) for i, j in up]
        last = lax.slice_in_dim(value, length - width, length, axis=dim)
        initial = lax.slice_in_dim(value, 0, width, axis=dim)
        before = lax.ppermute(last, axis, up)
        after = lax.ppermute(initial, axis, down)
        value = jnp.concatenate([before, value, after], axis=dim)
    return value


def temporal_sum(cached, current, temporal_w):
    frames = current.shape[0]
    joined = jnp.concatenate([cached, current], 0)
    total = jnp.dot(joined[0:frames], temporal_w[0], preferred_element_type=jnp.float32)
    total = total + jnp.dot(
        joined[1 : frames + 1], temporal_w[1], preferred_element_type=jnp.float32
    )
    return total + jnp.dot(
        joined[2 : frames + 2], temporal_w[2], preferred_element_type=jnp.float32
    )


def finish(down, temporal, bias_mid, norm_gain, latent_proj):
    block = down.astype(jnp.float32) + bias_mid + temporal
    scale = lax.rsqrt(jnp.mean(block * block, axis=-1, keepdims=True) + 1e-06)
    normed = (block * scale * norm_gain).astype(jnp.bfloat16)
    return jnp.dot(normed, latent_proj, preferred_element_type=jnp.float32)


def shards(
    features,
    conv_in,
    bias_in,
    down_proj,
    bias_down,
    spatial_w,
    temporal_w,
    bias_mid,
    norm_gain,
    latent_proj,
):
    cached = shifted(features, "tm", 1)
    joined = jnp.concatenate([cached, features], 0)
    extended = with_halo(joined, (("rows", 1),), 1)
    conv1 = lax.conv_general_dilated(
        extended[None],
        conv_in,
        (1, 1, 1),
        ((0, 0), (0, 0), (1, 1)),
        dimension_numbers=("NDHWC", "DHWIO", "NDHWC"),
        preferred_element_type=jnp.float32,
    )[0]
    hidden = jax.nn.silu(conv1 + bias_in).astype(jnp.bfloat16)
    frames, height, width, chans = hidden.shape
    patches = hidden.reshape(frames, height // 2, 2, width // 2, 2, chans).transpose(
        0, 1, 3, 2, 4, 5
    )
    patches = patches.reshape(frames, height // 2, width // 2, 4 * chans)
    down_flat = down_proj.reshape(4 * chans, down_proj.shape[3])
    down = (jnp.dot(patches, down_flat, preferred_element_type=jnp.float32) + bias_down).astype(
        jnp.bfloat16
    )
    act = jax.nn.silu(down.astype(jnp.float32)).astype(jnp.bfloat16)
    edged_act = with_halo(act, (("rows", 1),), 1)
    spatial = lax.conv_general_dilated(
        edged_act,
        spatial_w,
        (1, 1),
        ((0, 0), (1, 1)),
        dimension_numbers=("NHWC", "HWIO", "NHWC"),
        preferred_element_type=jnp.float32,
    ).astype(jnp.bfloat16)
    previous = shifted(spatial[-2:], "tm", 1)
    latent = finish(
        down, temporal_sum(previous, spatial, temporal_w), bias_mid, norm_gain, latent_proj
    )
    moved = latent.transpose(0, 3, 1, 2)
    tokens = lax.all_to_all(moved, "rows", split_axis=3, concat_axis=2, tiled=True)
    return tokens.transpose(0, 3, 1, 2)


def solution(mesh):
    return jax.shard_map(
        shards,
        mesh=mesh,
        in_specs=(P("tm", "rows", None, None), P(), P(), P(), P(), P(), P(), P(), P(), P()),
        out_specs=P("tm", "rows", None, None),
        check_vma=False,
    )
```

profile of v0, /device:TPU:2, one launch (start us, length us, event | category | flops | bytes accessed | tf_op | source)
XLA Modules:
  0.0 100.7 jit_solution(478879311481211961)
XLA Ops:
  0.0 2.0 %collective-permute-start = (bf16[2,2,384,128]{3,2,1,0:T(8,128)(2,1)}, bf16[2,2,384,128]{3,2,1,0:T(8,128)(2,1)S(1)}, u32[]{:S(2)}, u32[]{:S(2)}) collective-permute-start(bf16[2,2,384,128]{3,2,1,0:T(8,128)(2,1)} %param.10), channel_id=1, source_target_pairs={{0,64},{64,128},{128,192},{192,256},{256,320},{320,384},{384,448},... | collective-permute-start | bytes 1179656 | tf_op jit(solution)/shard_map/ppermute | solution.py:10
  2.1 7.4 %collective-permute-done = bf16[2,2,384,128]{3,2,1,0:T(8,128)(2,1)S(1)} collective-permute-done((bf16[2,2,384,128]{3,2,1,0:T(8,128)(2,1)}, bf16[2,2,384,128]{3,2,1,0:T(8,128)(2,1)S(1)}, u32[]{:S(2)}, u32[]{:S(2)}) %collective-permute-start) | collective-permute-done | bytes 393248 | tf_op jit(solution)/shard_map/ppermute | solution.py:10
  9.5 1.1 %constant_dynamic-update-slice_fusion = bf16[4,2,384,128]{3,2,1,0:T(8,128)(2,1)S(1)} fusion(bf16[4,2,384,128]{3,2,1,0:T(8,128)(2,1)S(1)} %constant_dynamic-update-slice_fusion.1, bf16[2,2,384,128]{3,2,1,0:T(8,128)(2,1)} %param.10), kind=kLoop, calls=%fused_computation.50 | loop fusion | bytes 786432 | tf_op jit(solution)/shard_map/concatenate | solution.py:58
  10.6 3.5 %collective-permute-start.1 = (bf16[4,1,384,128]{3,2,1,0:T(8,128)(2,1)S(1)}, bf16[4,1,384,128]{3,2,1,0:T(8,128)(2,1)S(1)}, u32[]{:S(2)}, u32[]{:S(2)}) collective-permute-start(bf16[4,1,384,128]{3,2,1,0:T(8,128)(2,1)S(1)} %get-tuple-element.5), channel_id=1, source_target_pairs={{0,1},{1,2},{2,3},{3,4},{4,5},{5,6},{6,7},{7,8},{8,9},{9,10},{10,1... | collective-permute-start | bytes 1179656 | tf_op jit(solution)/shard_map/ppermute | solution.py:20
  14.1 1.3 %collective-permute-start.2 = (bf16[4,1,384,128]{3,2,1,0:T(8,128)(2,1)S(1)}, bf16[4,1,384,128]{3,2,1,0:T(8,128)(2,1)S(1)}, u32[]{:S(2)}, u32[]{:S(2)}) collective-permute-start(bf16[4,1,384,128]{3,2,1,0:T(8,128)(2,1)S(1)} %get-tuple-element.6), channel_id=1, source_target_pairs={{1,0},{2,1},{3,2},{4,3},{5,4},{6,5},{7,6},{8,7},{9,8},{10,9},{11,1... | collective-permute-start | bytes 1179656 | tf_op jit(solution)/shard_map/ppermute | solution.py:21
  15.4 6.4 %collective-permute-done.1 = bf16[4,1,384,128]{3,2,1,0:T(8,128)(2,1)S(1)} collective-permute-done((bf16[4,1,384,128]{3,2,1,0:T(8,128)(2,1)S(1)}, bf16[4,1,384,128]{3,2,1,0:T(8,128)(2,1)S(1)}, u32[]{:S(2)}, u32[]{:S(2)}) %collective-permute-start.1) | collective-permute-done | bytes 393248 | tf_op jit(solution)/shard_map/ppermute | solution.py:20
  21.8 4.1 %collective-permute-done.2 = bf16[4,1,384,128]{3,2,1,0:T(8,128)(2,1)S(1)} collective-permute-done((bf16[4,1,384,128]{3,2,1,0:T(8,128)(2,1)S(1)}, bf16[4,1,384,128]{3,2,1,0:T(8,128)(2,1)S(1)}, u32[]{:S(2)}, u32[]{:S(2)}) %collective-permute-start.2) | collective-permute-done | bytes 393248 | tf_op jit(solution)/shard_map/ppermute | solution.py:21
  26.1 1.2 %copy.59 = bf16[4,4,1,384,128]{4,1,3,0,2:T(4,128)(2,1)S(1)} copy(bf16[4,4,1,384,128]{4,3,1,0,2:T(8,128)(2,1)S(1)} %maximum_bitcast_fusion) | data formatting | bytes 3145728
  27.4 0.6 pad.clone
  28.0 0.2 copy.47
  28.3 0.9 copy-done.8
  29.2 3.1 %fusion.8 = f32[2,2,8,49,128]{4,2,3,1,0:T(8,128)S(1)} fusion(bf16[3,3,3,128,128]{4,3,2,1,0:T(8,128)(2,1)S(1)} %copy-done.8, bf16[4,4,1,7,2,128]{5,3,4,1,0,2:T(8,128)(2,1)S(1)} %slice.30, bf16[4,4,1,8,49,128]{5,3,4,1,0,2:T(8,128)(2,1)S(1)} %copy.47, pred[8,49]{0,1:T(8,128)(4,1)S(1)} %copy-done.9), kind=kOutput, calls=%fused_computation.10 | convolution fusion | flops 1392480256 | bytes 3350920 | tf_op jit(solution)/shard_map/conv_general_dilated | solution.py:60
  32.3 0.4 copy.48
  32.9 0.2 fusion.20
  33.2 0.4 copy.51
  33.7 0.3 fusion.15
  34.1 1.3 %collective-permute-start.4 = (bf16[2,1,192,256]{3,2,0,1:T(8,128)(2,1)S(1)}, bf16[2,1,192,256]{3,2,0,1:T(8,128)(2,1)S(1)}, u32[]{:S(2)}, u32[]{:S(2)}) collective-permute-start(bf16[2,1,192,256]{3,2,0,1:T(8,128)(2,1)S(1)} %fusion.30), channel_id=1, source_target_pairs={{1,0},{2,1},{3,2},{4,3},{5,4},{6,5},{7,6},{8,7},{9,8},{10,9},{11,1... | collective-permute-start | bytes 589832 | tf_op jit(solution)/shard_map/ppermute | solution.py:21
  35.4 4.6 %collective-permute-start.3 = (bf16[2,1,192,256]{3,2,0,1:T(8,128)(2,1)S(1)}, bf16[2,1,192,256]{3,2,0,1:T(8,128)(2,1)S(1)}, u32[]{:S(2)}, u32[]{:S(2)}) collective-permute-start(bf16[2,1,192,256]{3,2,0,1:T(8,128)(2,1)S(1)} %fusion.30), channel_id=1, source_target_pairs={{0,1},{1,2},{2,3},{3,4},{4,5},{5,6},{6,7},{7,8},{8,9},{9,10},{10,1... | collective-permute-start | bytes 589832 | tf_op jit(solution)/shard_map/ppermute | solution.py:20
  40.0 1.7 %collective-permute-done.4 = bf16[2,1,192,256]{3,2,0,1:T(8,128)(2,1)S(1)} collective-permute-done((bf16[2,1,192,256]{3,2,0,1:T(8,128)(2,1)S(1)}, bf16[2,1,192,256]{3,2,0,1:T(8,128)(2,1)S(1)}, u32[]{:S(2)}, u32[]{:S(2)}) %collective-permute-start.4) | collective-permute-done | bytes 196640 | tf_op jit(solution)/shard_map/ppermute | solution.py:21
  41.7 1.5 %collective-permute-done.3 = bf16[2,1,192,256]{3,2,0,1:T(8,128)(2,1)S(1)} collective-permute-done((bf16[2,1,192,256]{3,2,0,1:T(8,128)(2,1)S(1)}, bf16[2,1,192,256]{3,2,0,1:T(8,128)(2,1)S(1)}, u32[]{:S(2)}, u32[]{:S(2)}) %collective-permute-start.3) | collective-permute-done | bytes 196640 | tf_op jit(solution)/shard_map/ppermute | solution.py:20
  43.2 0.6 copy.60
  43.9 0.5 pad.2.clone
  44.4 0.6 fusion.17
  45.0 0.7 fusion.13
  45.9 1.9 %collective-permute-start.5 = (bf16[2,1,192,256]{3,2,0,1:T(8,128)(2,1)S(1)}, bf16[2,1,192,256]{3,2,0,1:T(8,128)(2,1)S(1)}, u32[]{:S(2)}, u32[]{:S(2)}) collective-permute-start(bf16[2,1,192,256]{3,2,0,1:T(8,128)(2,1)S(1)} %slice_bitcast_fusion), channel_id=1, source_target_pairs={{0,64},{64,128},{128,192},{192,256},{256,320},{320,384},{384,448},... | collective-permute-start | bytes 589832 | tf_op jit(solution)/shard_map/ppermute | solution.py:10
  47.8 0.2 fusion.25
  48.0 4.8 %collective-permute-done.5 = bf16[2,1,192,256]{3,2,0,1:T(8,128)(2,1)S(1)} collective-permute-done((bf16[2,1,192,256]{3,2,0,1:T(8,128)(2,1)S(1)}, bf16[2,1,192,256]{3,2,0,1:T(8,128)(2,1)S(1)}, u32[]{:S(2)}, u32[]{:S(2)}) %collective-permute-start.5) | collective-permute-done | bytes 196640 | tf_op jit(solution)/shard_map/ppermute | solution.py:10
  52.8 0.2 fusion.22
  53.1 0.4 multiply_reduce_fusion
  53.5 0.2 convolution_bitcast_fusion
  53.8 46.1 %all_to_all.12 = f32[2,16,1,192]{1,0,2,3:T(2,128)S(1)} all-to-all(f32[2,16,1,192]{1,0,2,3:T(2,128)S(1)} %copy.55), channel_id=1, replica_groups=mesh['tm'=8,'rows'=64] {'rows'}, dimensions={3} | all-to-all | bytes 49152 | tf_op jit(solution)/shard_map/all_to_all | solution.py:93
  99.9 0.8 copy.56
  (35 shorter events, 1.2 us)
Async XLA Ops:
  0.0 45.0 %copy-start = (bf16[3,3,256,256]{3,2,1,0:T(8,128)(2,1)S(1)}, bf16[3,3,256,256]{3,2,1,0:T(8,128)(2,1)}, u32[]{:S(2)}) copy-start(bf16[3,3,256,256]{3,2,1,0:T(8,128)(2,1)} %param.15) | copy-start | bytes 3538948
  0.0 9.4 %collective-permute-start = (bf16[2,2,384,128]{3,2,1,0:T(8,128)(2,1)}, bf16[2,2,384,128]{3,2,1,0:T(8,128)(2,1)S(1)}, u32[]{:S(2)}, u32[]{:S(2)}) collective-permute-start(bf16[2,2,384,128]{3,2,1,0:T(8,128)(2,1)} %param.10), channel_id=1, source_target_pairs={{0,64},{64,128},{128,192},{192,256},{256,320},{320,384},{384,448},... | collective-permute-start | bytes 1179656 | tf_op jit(solution)/shard_map/ppermute | solution.py:10
  10.6 11.2 %collective-permute-start.1 = (bf16[4,1,384,128]{3,2,1,0:T(8,128)(2,1)S(1)}, bf16[4,1,384,128]{3,2,1,0:T(8,128)(2,1)S(1)}, u32[]{:S(2)}, u32[]{:S(2)}) collective-permute-start(bf16[4,1,384,128]{3,2,1,0:T(8,128)(2,1)S(1)} %get-tuple-element.5), channel_id=1, source_target_pairs={{0,1},{1,2},{2,3},{3,4},{4,5},{5,6},{6,7},{7,8},{8,9},{9,10},{10,1... | collective-permute-start | bytes 1179656 | tf_op jit(solution)/shard_map/ppermute | solution.py:20
  14.1 11.9 %collective-permute-start.2 = (bf16[4,1,384,128]{3,2,1,0:T(8,128)(2,1)S(1)}, bf16[4,1,384,128]{3,2,1,0:T(8,128)(2,1)S(1)}, u32[]{:S(2)}, u32[]{:S(2)}) collective-permute-start(bf16[4,1,384,128]{3,2,1,0:T(8,128)(2,1)S(1)} %get-tuple-element.6), channel_id=1, source_target_pairs={{1,0},{2,1},{3,2},{4,3},{5,4},{6,5},{7,6},{8,7},{9,8},{10,9},{11,1... | collective-permute-start | bytes 1179656 | tf_op jit(solution)/shard_map/ppermute | solution.py:21
  28.0 1.2 %copy-start.8 = (bf16[3,3,3,128,128]{4,3,2,1,0:T(8,128)(2,1)S(1)}, bf16[3,3,3,128,128]{4,3,2,1,0:T(8,128)(2,1)}, u32[]{:S(2)}) copy-start(bf16[3,3,3,128,128]{4,3,2,1,0:T(8,128)(2,1)} %param.11) | copy-start | bytes 2654212
  28.0 1.2 %copy-start.9 = (pred[8,49]{0,1:T(8,128)(4,1)S(1)}, pred[8,49]{0,1:T(8,128)(4,1)}, u32[]{:S(2)}) copy-start(pred[8,49]{0,1:T(8,128)(4,1)} %constant.21) | copy-start | bytes 1180
  32.3 0.7 copy-start.7
  32.8 1.0 copy-start.2
  32.8 1.0 copy-start.4
  34.1 7.6 %collective-permute-start.4 = (bf16[2,1,192,256]{3,2,0,1:T(8,128)(2,1)S(1)}, bf16[2,1,192,256]{3,2,0,1:T(8,128)(2,1)S(1)}, u32[]{:S(2)}, u32[]{:S(2)}) collective-permute-start(bf16[2,1,192,256]{3,2,0,1:T(8,128)(2,1)S(1)} %fusion.30), channel_id=1, source_target_pairs={{1,0},{2,1},{3,2},{4,3},{5,4},{6,5},{7,6},{8,7},{9,8},{10,9},{11,1... | collective-permute-start | bytes 589832 | tf_op jit(solution)/shard_map/ppermute | solution.py:21
  35.4 7.7 %collective-permute-start.3 = (bf16[2,1,192,256]{3,2,0,1:T(8,128)(2,1)S(1)}, bf16[2,1,192,256]{3,2,0,1:T(8,128)(2,1)S(1)}, u32[]{:S(2)}, u32[]{:S(2)}) collective-permute-start(bf16[2,1,192,256]{3,2,0,1:T(8,128)(2,1)S(1)} %fusion.30), channel_id=1, source_target_pairs={{0,1},{1,2},{2,3},{3,4},{4,5},{5,6},{6,7},{7,8},{8,9},{9,10},{10,1... | collective-permute-start | bytes 589832 | tf_op jit(solution)/shard_map/ppermute | solution.py:20
  43.8 1.1 %copy-start.10 = (pred[16,25]{0,1:T(8,128)(4,1)S(1)}, pred[16,25]{0,1:T(8,128)(4,1)}, u32[]{:S(2)}) copy-start(pred[16,25]{0,1:T(8,128)(4,1)} %constant.22) | copy-start | bytes 1204
  45.0 2.8 %copy-start.1 = (bf16[3,256,256]{2,1,0:T(8,128)(2,1)S(1)}, bf16[3,256,256]{2,1,0:T(8,128)(2,1)}, u32[]{:S(2)}) copy-start(bf16[3,256,256]{2,1,0:T(8,128)(2,1)} %param.16) | copy-start | bytes 1179652
  45.7 7.4 %copy-start.5 = (f32[256]{0:T(256)S(1)}, f32[256]{0:T(256)}, u32[]{:S(2)}) copy-start(f32[256]{0:T(256)} %param.17) | copy-start | bytes 3076
  45.9 7.0 %collective-permute-start.5 = (bf16[2,1,192,256]{3,2,0,1:T(8,128)(2,1)S(1)}, bf16[2,1,192,256]{3,2,0,1:T(8,128)(2,1)S(1)}, u32[]{:S(2)}, u32[]{:S(2)}) collective-permute-start(bf16[2,1,192,256]{3,2,0,1:T(8,128)(2,1)S(1)} %slice_bitcast_fusion), channel_id=1, source_target_pairs={{0,64},{64,128},{128,192},{192,256},{256,320},{320,384},{384,448},... | collective-permute-start | bytes 589832 | tf_op jit(solution)/shard_map/ppermute | solution.py:10
  48.0 5.4 %copy-start.3 = (bf16[256,16]{0,1:T(8,128)(2,1)S(1)}, bf16[256,16]{0,1:T(8,128)(2,1)}, u32[]{:S(2)}) copy-start(bf16[256,16]{0,1:T(8,128)(2,1)} %param.19) | copy-start | bytes 24580
  48.0 5.4 %copy-start.6 = (f32[256]{0:T(256)S(1)}, f32[256]{0:T(256)}, u32[]{:S(2)}) copy-start(f32[256]{0:T(256)} %param.18) | copy-start | bytes 3076
where the time goes:
time: 101 us
  blocking collectives  46.1 us (46%)
  waiting for transfers between devices  25.9 us (26%)
  starting transfers between devices  14.6 us (14%)
  local copies, waits for them, and re-layouts  7.49 us (7%)
  matrix products  5.04 us (5%)
  other arithmetic  1.17 us (1%)
    all_to_all x1, blocking collectives, shards(): lax.all_to_all(moved, 'rows', split_axis=3, concat_axis=2, tiled=True)  46.1 us
    ppermute x2, waiting for transfers between devices, shifted(): return lax.ppermute(block, axis, route)  12.2 us
    ppermute x2, starting transfers between devices, with_halo(): before = lax.ppermute(last, axis, up)  8.06 us
    ppermute x2, waiting for transfers between devices, with_halo(): before = lax.ppermute(last, axis, up)  7.89 us
    ppermute x2, waiting for transfers between devices, with_halo(): after = lax.ppermute(initial, axis, down)  5.83 us
    ppermute x2, starting transfers between devices, shifted(): return lax.ppermute(block, axis, route)  3.96 us
    conv_general_dilated x1, matrix products, shards(): lax.conv_general_dilated(extended[None], conv_in, (1, 1, 1), ((0, 0), (0,...  3.11 us
    unnamed x25, local copies, waits for them, and re-layouts  2.96 us
  transfers between devices with their start and end apart: 6, of which 6 were waited for; matrix products, arithmetic and copies ran while one was open for 0% of the time, Pallas kernels for 0%

commit v1 on v0

v1 whole, which is shorter than its diff:
```python
import functools

import jax
import jax.numpy as jnp
from jax import lax
from jax.experimental import pallas as pl
from jax.experimental.pallas import tpu as pltpu
from jax.sharding import PartitionSpec as P

MESH = pl.DeviceIdType.MESH
F32 = jnp.float32
BF16 = jnp.bfloat16
PAD = 8


def silu(v):
    return v / (1.0 + jnp.exp(-v))


def remote(src, dst, send, recv, axis, peer):
    return pltpu.make_async_remote_copy(
        src_ref=src, dst_ref=dst, send_sem=send, recv_sem=recv, device_id={axis: peer}, device_id_type=MESH
    )


def kernel(
    sections, shards, feat, conv_in, bias_in, down_proj, bias_down, spatial_w, temporal_w, bias_mid, gain, proj_t, out,
    x, w1, w2, w3, w4, acc, act, acc2, sp, down, normed, projs, outbox, inbox,
    load_sem, own_sem, fs_send, fs_recv, as_send, as_recv, ss_send, ss_recv, a2a_send, a2a_recv, ready,
):
    tm, row = lax.axis_index("tm"), lax.axis_index("rows")
    width, lat = feat.shape[2], down.shape[1]
    chans = proj_t.shape[0]
    per = lat // shards
    above, below = lax.rem(row + shards - 1, shards), lax.rem(row + 1, shards)
    later, earlier = lax.rem(tm + 1, sections), lax.rem(tm + sections - 1, sections)
    even = lax.rem(tm, 2) == 0
    has_above, has_below = row > 0, row < shards - 1
    has_prev, has_next = tm > 0, tm < sections - 1

    barrier = pltpu.get_barrier_semaphore()
    for axis, peer in (("rows", above), ("rows", below), ("tm", later), ("tm", earlier)):
        pl.semaphore_signal(barrier, inc=1, device_id={axis: peer}, device_id_type=MESH)

    own = pltpu.make_async_copy(feat, x.at[pl.ds(2, 2), pl.ds(1, 2)], own_sem)
    own.start()
    loads = [
        pltpu.make_async_copy(src, dst, load_sem.at[i])
        for i, (src, dst) in enumerate(((conv_in, w1), (down_proj, w2), (spatial_w, w3), (temporal_w, w4)))
    ]
    for load in loads:
        load.start()

    pl.semaphore_wait(barrier, 4)

    def pair(slot, frame):
        return fs_send.at[slot, frame], fs_recv.at[slot, frame]

    to_next = [remote(feat.at[f], x.at[f, pl.ds(1, 2)], *pair(2, f), "tm", later) for f in range(2)]
    to_below = [remote(feat.at[f, 1], x.at[2 + f, 0], *pair(0, f), "rows", below) for f in range(2)]
    to_above = [remote(feat.at[f, 0], x.at[2 + f, 3], *pair(1, f), "rows", above) for f in range(2)]
    relay_below = [remote(x.at[f, 2], x.at[f, 0], *pair(3, f), "rows", below) for f in range(2)]
    relay_above = [remote(x.at[f, 1], x.at[f, 3], *pair(4, f), "rows", above) for f in range(2)]
    pass_top = [remote(x.at[2 + f, 0], x.at[f, 0], fs_send.at[5, f], fs_recv.at[3, f], "tm", later) for f in range(2)]
    pass_bottom = [remote(x.at[2 + f, 3], x.at[f, 3], fs_send.at[6, f], fs_recv.at[4, f], "tm", later) for f in range(2)]

    for f in range(2):
        pl.when(has_next)(to_next[f].start)
        pl.when(has_below)(to_below[f].start)
        pl.when(has_above)(to_above[f].start)

    step, distance = 0, 1
    while distance <= shards // 4:
        for peer in (lax.rem(row + distance, shards), lax.rem(row + shards - distance, shards)):
            pl.semaphore_signal(ready.at[step], inc=1, device_id={"rows": peer}, device_id_type=MESH)
        if step == 0:
            edge = jnp.zeros((PAD, x.shape[3]), F32)
            for c in range(3):
                for f in range(2):
                    for o in range(2):
                        acc[c, f, o, pl.ds(0, PAD), :] = edge
                        acc[c, f, o, pl.ds(PAD + width, PAD), :] = edge
                    acc2[c, f, pl.ds(0, PAD), :] = jnp.zeros((PAD, acc2.shape[3]), F32)
                    acc2[c, f, pl.ds(PAD + lat, PAD), :] = jnp.zeros((PAD, acc2.shape[3]), F32)
            projs[...] = jnp.zeros(projs.shape, BF16)
            for s in range(2 * per):
                projs[s, pl.ds(chans * s, chans), :] = proj_t[...]

            @pl.when(jnp.logical_not(has_prev))
            def _():
                x[pl.ds(0, 2)] = jnp.zeros((2,) + x.shape[1:], BF16)
                sp[pl.ds(0, 2)] = jnp.zeros((2,) + sp.shape[1:], BF16)

            @pl.when(jnp.logical_not(has_above))
            def _():
                for f in range(4):
                    x[f, 0] = jnp.zeros(x.shape[2:], BF16)
                for f in range(2):
                    act[f, 0] = jnp.zeros(act.shape[2:], BF16)

            @pl.when(jnp.logical_not(has_below))
            def _():
                for f in range(4):
                    x[f, 3] = jnp.zeros(x.shape[2:], BF16)
                for f in range(2):
                    act[f, 2] = jnp.zeros(act.shape[2:], BF16)
        pl.semaphore_wait(ready.at[step], 2)
        step, distance = step + 1, distance * 2

    both = jnp.logical_and
    relays = both(even, has_prev)
    for f in range(2):
        pl.when(has_prev)(to_next[f].wait_recv)
        pl.when(both(relays, has_below))(relay_below[f].start)
        pl.when(both(relays, has_above))(relay_above[f].start)
    for f in range(2):
        pl.when(has_above)(to_below[f].wait_recv)
        pl.when(both(even, has_above))(pass_top[f].start)
        pl.when(has_below)(to_above[f].wait_recv)
        pl.when(both(even, has_below))(pass_bottom[f].start)
    own.wait()
    loads[0].wait()

    def window(frames, o):
        return jnp.concatenate([x[f, o + b] for f in frames for b in range(3)], axis=-1)

    def taps(steps):
        return jnp.concatenate(
            [jnp.concatenate([w1[a, b, c] for c in range(3)], axis=-1) for a in steps for b in range(3)], axis=0
        )

    def conv(f, frames, steps, first):
        weights = taps(steps)
        for o in range(2):
            total = jnp.dot(window(frames, o), weights, preferred_element_type=F32)
            for c in range(3):
                part = total[:, c * 128 : (c + 1) * 128]
                rows = (c, f, o, pl.ds(PAD, width))
                acc[rows] = part if first else acc[rows] + part

    conv(0, (2,), (2,), True)
    conv(1, (2, 3), (1, 2), True)
    for f in range(2):
        pl.when(both(has_prev, has_above))(relay_below[f].wait_recv)
        pl.when(both(has_prev, has_below))(relay_above[f].wait_recv)
    conv(0, (0, 1), (0, 1), False)
    conv(1, (1,), (0,), False)

    loads[1].wait()
    down_w = w2[...].reshape(4 * w2.shape[2], w2.shape[3])
    act_below = [remote(act.at[f, 1], act.at[f, 0], as_send.at[0, f], as_recv.at[0, f], "rows", below) for f in range(2)]
    act_above = [remote(act.at[f, 1], act.at[f, 2], as_send.at[1, f], as_recv.at[1, f], "rows", above) for f in range(2)]
    for f in range(2):
        parts = []
        for o in range(2):
            for b in range(2):
                v = bias_in[...][None, :]
                for c in range(3):
                    v = v + acc[c, f, o, pl.ds(PAD - 1 + b + c, lat, stride=2), :]
                parts.append(silu(v).astype(BF16))
        d = jnp.dot(jnp.concatenate(parts, axis=-1), down_w, preferred_element_type=F32)
        d = (d + bias_down[...][None, :]).astype(BF16)
        down[f] = d
        act[f, 1] = silu(d.astype(F32)).astype(BF16)
        pl.when(has_below)(act_below[f].start)
        pl.when(has_above)(act_above[f].start)

    loads[2].wait()
    to_later = [remote(sp.at[2 + f], sp.at[f], ss_send.at[f], ss_recv.at[f], "tm", later) for f in range(2)]

    def spatial(f, b, first):
        weights = jnp.concatenate([w3[b, c] for c in range(3)], axis=-1)
        total = jnp.dot(act[f, b], weights, preferred_element_type=F32)
        size = w3.shape[3]
        for c in range(3):
            part = total[:, c * size : (c + 1) * size]
            rows = (c, f, pl.ds(PAD, lat))
            acc2[rows] = part if first else acc2[rows] + part

    for f in range(2):
        spatial(f, 1, True)
    for f in range(2):
        pl.when(has_above)(act_below[f].wait_recv)
        spatial(f, 0, False)
        pl.when(has_below)(act_above[f].wait_recv)
        spatial(f, 2, False)
        v = acc2[0, f, pl.ds(PAD - 1, lat), :]
        for c in (1, 2):
            v = v + acc2[c, f, pl.ds(PAD - 1 + c, lat), :]
        sp[2 + f] = v.astype(BF16)
        pl.when(has_next)(to_later[f].start)

    loads[3].wait()

    def mixed(frame, step):
        return jnp.dot(sp[frame], w4[step], preferred_element_type=F32)

    local = [mixed(2, 2), mixed(3, 2) + mixed(2, 1)]
    for f in range(2):
        pl.when(has_prev)(to_later[f].wait_recv)
    half = normed.shape[3]
    for f in range(2):
        block = down[f].astype(F32) + bias_mid[...][None, :] + local[f]
        block = block + (mixed(0, 0) + mixed(1, 1) if f == 0 else mixed(1, 0))
        scale = lax.rsqrt(jnp.mean(block * block, axis=-1, keepdims=True) + 1e-06)
        value = block * scale * gain[...][None, :]
        for h in range(2):
            normed[f, h] = value[:, h * half : (h + 1) * half]

    total = None
    for f in range(2):
        for c in range(per):
            rows = jnp.concatenate(
                [normed[f, h, pl.ds(c, shards, stride=per), :] for h in range(2)], axis=-1
            ).astype(BF16)
            part = lax.dot_general(
                rows, projs[f * per + c], (((1,), (1,)), ((), ())), preferred_element_type=F32
            )
            total = part if total is None else total + part
    outbox[...] = total[:, None, :]

    def token(peer, source):
        return remote(outbox.at[peer], inbox.at[source], a2a_send.at[peer], a2a_recv.at[source], "rows", peer)

    middle = shards // 2
    token(lax.rem(row + middle, shards), row).start()

    def launch(k, carry):
        token(lax.rem(row + middle - k, shards), row).start()
        token(lax.rem(row + middle + k, shards), row).start()
        return carry

    lax.fori_loop(1, middle, launch, 0)
    inbox[row] = outbox[row]

    for f in range(2):
        pl.when(has_next)(to_next[f].wait_send)
        pl.when(has_next)(to_later[f].wait_send)
        for ok, copies in (
            (has_below, (to_below[f], act_below[f])),
            (has_above, (to_above[f], act_above[f])),
            (both(relays, has_below), (relay_below[f],)),
            (both(relays, has_above), (relay_above[f],)),
            (both(even, has_above), (pass_top[f],)),
            (both(even, has_below), (pass_bottom[f],)),
        ):
            for copy in copies:
                pl.when(ok)(copy.wait_send)

    def land(k, carry):
        peer = lax.rem(row + k, shards)
        token(peer, peer).wait_recv()
        return carry

    def leave(k, carry):
        peer = lax.rem(row + k, shards)
        token(peer, peer).wait_send()
        return carry

    lax.fori_loop(1, shards, land, 0)
    out[...] = jnp.transpose(inbox[:, 0, :])[: 2 * per * chans, :]
    lax.fori_loop(1, shards, leave, 0)


def shards_fn(
    sections, shards, features, conv_in, bias_in, down_proj, bias_down, spatial_w, temporal_w, bias_mid, norm_gain, latent_proj
):
    frames, height, width, c1 = features.shape
    lat, c2 = width // 2, down_proj.shape[3]
    chans = latent_proj.shape[1]
    per = lat // shards
    hbm = pl.BlockSpec(memory_space=pl.ANY)
    vmem = pl.BlockSpec(memory_space=pltpu.VMEM)
    dma = pltpu.SemaphoreType.DMA
    tokens = pl.pallas_call(
        functools.partial(kernel, sections, shards),
        out_shape=jax.ShapeDtypeStruct((frames * per * chans, shards), F32),
        in_specs=[hbm, hbm, vmem, hbm, vmem, hbm, hbm, vmem, vmem, vmem],
        out_specs=vmem,
        scratch_shapes=[
            pltpu.VMEM((4, 4, width, c1), BF16),
            pltpu.VMEM(conv_in.shape, BF16),
            pltpu.VMEM(down_proj.shape, BF16),
            pltpu.VMEM(spatial_w.shape, BF16),
            pltpu.VMEM(temporal_w.shape, BF16),
            pltpu.VMEM((3, 2, 2, width + 2 * PAD, c1), F32),
            pltpu.VMEM((2, 3, lat, c2), BF16),
            pltpu.VMEM((3, 2, lat + 2 * PAD, c2), F32),
            pltpu.VMEM((4, lat, c2), BF16),
            pltpu.VMEM((2, lat, c2), BF16),
            pltpu.VMEM((2, 2, lat, c2 // 2), F32),
            pltpu.VMEM((2 * per, 128, c2), BF16),
            pltpu.VMEM((shards, 1, 128), F32),
            pltpu.VMEM((shards, 1, 128), F32),
            dma((4,)),
            dma,
            dma((7, 2)),
            dma((5, 2)),
            dma((2, 2)),
            dma((2, 2)),
            dma((2,)),
            dma((2,)),
            dma((shards,)),
            dma((shards,)),
            pltpu.SemaphoreType.REGULAR((8,)),
        ],
        compiler_params=pltpu.CompilerParams(collective_id=0, has_side_effects=True, vmem_limit_bytes=67_043_328),
        name="encoder",
    )(features, conv_in, bias_in, down_proj, bias_down, spatial_w, temporal_w, bias_mid, norm_gain, latent_proj.T)
    return tokens.reshape(frames, per, chans, shards)


def solution(mesh):
    sizes = mesh.shape
    return jax.shard_map(
        functools.partial(shards_fn, sizes["tm"], sizes["rows"]),
        mesh=mesh,
        in_specs=(P("tm", "rows", None, None), P(), P(), P(), P(), P(), P(), P(), P(), P()),
        out_specs=P("tm", "rows", None, None),
        check_vma=False,
    )
```

time: 101 us -> 51.9 us (0.51)
  the two profiles are of different devices: /device:TPU:2 before, /device:TPU:6 now
where the time goes in v1:
time: 51.9 us; the launch traced here: 51.3 us
  Pallas kernels  49.9 us (96%)
  local copies, waits for them, and re-layouts  1.42 us (3%)
    pallas_call x1, Pallas kernels, shards_fn(): pl.pallas_call(functools.partial(kernel, sections, shards), out_shape=jax...  49.9 us
    unnamed x1, local copies, waits for them, and re-layouts  1.42 us

profile of v1, /device:TPU:6, one launch (start us, length us, event | category | flops | bytes accessed | tf_op | source)
XLA Modules:
  0.0 51.3 jit_solution(1127483479806155099)
XLA Ops:
  0.0 49.9 %encoder.1 = f32[96,64]{1,0:T(8,128)} custom-call(bf16[2,2,384,128]{3,2,1,0:T(8,128)(2,1)} %feat.1, bf16[3,3,3,128,128]{4,3,2,1,0:T(8,128)(2,1)} %conv_in.1, f32[128]{0:T(128)} %bias_in.1, bf16[2,2,128,256]{3,2,1,0:T(8,128)(2,1)} %down_proj.1, f32[256]{0:T(256)} %bias_down.1, bf16[3,3,256,256]{3,2,1,0:T(8,128)(2,1)} %spatial_w.1, ...), custom_call_target="tpu_custom_call" | custom-call | tf_op jit(solution)/shard_map/encoder/pallas_call | solution.py:275
  49.9 1.4 %copy.12 = f32[2,3,16,64]{3,2,1,0:T(8,128)} copy(f32[2,3,16,64]{3,2,1,0:T(8,128)} %bitcast.2) | data formatting | bytes 49152

commit v2 on v1

--- a/solution.py
+++ b/solution.py
@@ -24,8 +24,8 @@
 
 
 def kernel(
-    sections, shards, feat, conv_in, bias_in, down_proj, bias_down, spatial_w, temporal_w, bias_mid, gain, proj_t, out,
-    x, w1, w2, w3, w4, acc, act, acc2, sp, down, normed, projs, outbox, inbox,
+    sections, shards, feat, conv_in, bias_in_h, down_proj, bias_down_h, spatial_w, temporal_w, bias_mid_h, gain_h, proj_h, out,
+    x, w1, w2, w3, w4, bias_in, bias_down, bias_mid, gain, proj_t, acc, act, acc2, sp, down, normed, projs, outbox, inbox,
     load_sem, own_sem, fs_send, fs_recv, as_send, as_recv, ss_send, ss_recv, a2a_send, a2a_recv, ready,
 ):
     tm, row = lax.axis_index("tm"), lax.axis_index("rows")
@@ -46,10 +46,44 @@
     own.start()
     loads = [
         pltpu.make_async_copy(src, dst, load_sem.at[i])
-        for i, (src, dst) in enumerate(((conv_in, w1), (down_proj, w2), (spatial_w, w3), (temporal_w, w4)))
+        for i, (src, dst) in enumerate(
+            (
+                (conv_in, w1), (down_proj, w2), (spatial_w, w3), (temporal_w, w4), (bias_in_h, bias_in),
+                (bias_down_h, bias_down), (bias_mid_h, bias_mid), (gain_h, gain), (proj_h, proj_t),
+            )
+        )
     ]
     for load in loads:
         load.start()
+
+    edge = jnp.zeros((PAD, x.shape[3]), F32)
+    for c in range(3):
+        for f in range(2):
+            for o in range(2):
+                acc[c, f, o, pl.ds(0, PAD), :] = edge
+                acc[c, f, o, pl.ds(PAD + width, PAD), :] = edge
+            acc2[c, f, pl.ds(0, PAD), :] = jnp.zeros((PAD, acc2.shape[3]), F32)
+            acc2[c, f, pl.ds(PAD + lat, PAD), :] = jnp.zeros((PAD, acc2.shape[3]), F32)
+    projs[...] = jnp.zeros(projs.shape, BF16)
+
+    @pl.when(jnp.logical_not(has_prev))
+    def _():
+        x[pl.ds(0, 2)] = jnp.zeros((2,) + x.shape[1:], BF16)
+        sp[pl.ds(0, 2)] = jnp.zeros((2,) + sp.shape[1:], BF16)
+
+    @pl.when(jnp.logical_not(has_above))
+    def _():
+        for f in range(4):
+            x[f, 0] = jnp.zeros(x.shape[2:], BF16)
+        for f in range(2):
+            act[f, 0] = jnp.zeros(act.shape[2:], BF16)
+
+    @pl.when(jnp.logical_not(has_below))
+    def _():
+        for f in range(4):
+            x[f, 3] = jnp.zeros(x.shape[2:], BF16)
+        for f in range(2):
+            act[f, 2] = jnp.zeros(act.shape[2:], BF16)
 
     pl.semaphore_wait(barrier, 4)
 
@@ -69,43 +103,41 @@
         pl.when(has_below)(to_below[f].start)
         pl.when(has_above)(to_above[f].start)
 
-    step, distance = 0, 1
-    while distance <= shards // 4:
-        for peer in (lax.rem(row + distance, shards), lax.rem(row + shards - distance, shards)):
-            pl.semaphore_signal(ready.at[step], inc=1, device_id={"rows": peer}, device_id_type=MESH)
-        if step == 0:
-            edge = jnp.zeros((PAD, x.shape[3]), F32)
+    rounds = []
+    while 2 ** len(rounds) <= shards // 4:
+        rounds.append(2 ** len(rounds))
+
+    def tell(step):
+        if step < len(rounds):
+            for peer in (lax.rem(row + rounds[step], shards), lax.rem(row + shards - rounds[step], shards)):
+                pl.semaphore_signal(ready.at[step], inc=1, device_id={"rows": peer}, device_id_type=MESH)
+
+    def hear(step):
+        if step < len(rounds):
+            pl.semaphore_wait(ready.at[step], 2)
+            tell(step + 1)
+
+    tell(0)
+
+    def conv(f, frames, kept, first):
+        for o in range(2):
+            steps = [(n, n - f, b) for n in frames for b in kept[o]]
+            lhs = jnp.concatenate([x[n, o + b] for n, a, b in steps], axis=-1)
+            rhs = jnp.concatenate(
+                [jnp.concatenate([w1[a, b, c] for c in range(3)], axis=-1) for n, a, b in steps], axis=0
+            )
+            total = jnp.dot(lhs, rhs, preferred_element_type=F32)
             for c in range(3):
-                for f in range(2):
-                    for o in range(2):
-                        acc[c, f, o, pl.ds(0, PAD), :] = edge
-                        acc[c, f, o, pl.ds(PAD + width, PAD), :] = edge
-                    acc2[c, f, pl.ds(0, PAD), :] = jnp.zeros((PAD, acc2.shape[3]), F32)
-                    acc2[c, f, pl.ds(PAD + lat, PAD), :] = jnp.zeros((PAD, acc2.shape[3]), F32)
-            projs[...] = jnp.zeros(projs.shape, BF16)
-            for s in range(2 * per):
-                projs[s, pl.ds(chans * s, chans), :] = proj_t[...]
-
-            @pl.when(jnp.logical_not(has_prev))
-            def _():
-                x[pl.ds(0, 2)] = jnp.zeros((2,) + x.shape[1:], BF16)
-                sp[pl.ds(0, 2)] = jnp.zeros((2,) + sp.shape[1:], BF16)
-
-            @pl.when(jnp.logical_not(has_above))
-            def _():
-                for f in range(4):
-                    x[f, 0] = jnp.zeros(x.shape[2:], BF16)
-                for f in range(2):
-                    act[f, 0] = jnp.zeros(act.shape[2:], BF16)
-
-            @pl.when(jnp.logical_not(has_below))
-            def _():
-                for f in range(4):
-                    x[f, 3] = jnp.zeros(x.shape[2:], BF16)
-                for f in range(2):
-                    act[f, 2] = jnp.zeros(act.shape[2:], BF16)
-        pl.semaphore_wait(ready.at[step], 2)
-        step, distance = step + 1, distance * 2
+                part = total[:, c * 128 : (c + 1) * 128]
+                rows = (c, f, o, pl.ds(PAD, width))
+                acc[rows] = part if first else acc[rows] + part
+
+    held, halo = ((1, 2), (0, 1)), ((0,), (2,))
+    own.wait()
+    loads[0].wait()
+    conv(0, (2,), held, True)
+    conv(1, (2, 3), held, True)
+    hear(0)
 
     both = jnp.logical_and
     relays = both(even, has_prev)
@@ -113,44 +145,31 @@
         pl.when(has_prev)(to_next[f].wait_recv)
         pl.when(both(relays, has_below))(relay_below[f].start)
         pl.when(both(relays, has_above))(relay_above[f].start)
-    for f in range(2):
         pl.when(has_above)(to_below[f].wait_recv)
         pl.when(both(even, has_above))(pass_top[f].start)
         pl.when(has_below)(to_above[f].wait_recv)
         pl.when(both(even, has_below))(pass_bottom[f].start)
-    own.wait()
-    loads[0].wait()
-
-    def window(frames, o):
-        return jnp.concatenate([x[f, o + b] for f in frames for b in range(3)], axis=-1)
-
-    def taps(steps):
-        return jnp.concatenate(
-            [jnp.concatenate([w1[a, b, c] for c in range(3)], axis=-1) for a in steps for b in range(3)], axis=0
-        )
-
-    def conv(f, frames, steps, first):
-        weights = taps(steps)
-        for o in range(2):
-            total = jnp.dot(window(frames, o), weights, preferred_element_type=F32)
-            for c in range(3):
-                part = total[:, c * 128 : (c + 1) * 128]
-                rows = (c, f, o, pl.ds(PAD, width))
-                acc[rows] = part if first else acc[rows] + part
-
-    conv(0, (2,), (2,), True)
-    conv(1, (2, 3), (1, 2), True)
-    for f in range(2):
-        pl.when(both(has_prev, has_above))(relay_below[f].wait_recv)
-        pl.when(both(has_prev, has_below))(relay_above[f].wait_recv)
-    conv(0, (0, 1), (0, 1), False)
-    conv(1, (1,), (0,), False)
+    hear(1)
+    conv(0, (0, 1), held, False)
+    conv(0, (2,), halo, False)
+    hear(2)
+    conv(1, (1,), held, False)
+    conv(1, (2, 3), halo, False)
+    for load in loads[4:]:
+        load.wait()
+    for s in range(2 * per):
+        projs[s, pl.ds(chans * s, chans), :] = proj_t[...]
 
     loads[1].wait()
     down_w = w2[...].reshape(4 * w2.shape[2], w2.shape[3])
     act_below = [remote(act.at[f, 1], act.at[f, 0], as_send.at[0, f], as_recv.at[0, f], "rows", below) for f in range(2)]
     act_above = [remote(act.at[f, 1], act.at[f, 2], as_send.at[1, f], as_recv.at[1, f], "rows", above) for f in range(2)]
     for f in range(2):
+        for n in range(f, 2):
+            if n == 0 or f == 0:
+                pl.when(both(has_prev, has_above))(relay_below[n].wait_recv)
+                pl.when(both(has_prev, has_below))(relay_above[n].wait_recv)
+        conv(f, tuple(range(f, 2)), halo, False)
         parts = []
         for o in range(2):
             for b in range(2):
@@ -165,6 +184,7 @@
         pl.when(has_below)(act_below[f].start)
         pl.when(has_above)(act_above[f].start)
 
+    hear(3)
     loads[2].wait()
     to_later = [remote(sp.at[2 + f], sp.at[f], ss_send.at[f], ss_recv.at[f], "tm", later) for f in range(2)]
 
@@ -218,6 +238,8 @@
             )
             total = part if total is None else total + part
     outbox[...] = total[:, None, :]
+
+    hear(4)
 
     def token(peer, source):
         return remote(outbox.at[peer], inbox.at[source], a2a_send.at[peer], a2a_recv.at[source], "rows", peer)
@@ -275,7 +297,7 @@
     tokens = pl.pallas_call(
         functools.partial(kernel, sections, shards),
         out_shape=jax.ShapeDtypeStruct((frames * per * chans, shards), F32),
-        in_specs=[hbm, hbm, vmem, hbm, vmem, hbm, hbm, vmem, vmem, vmem],
+        in_specs=[hbm] * 10,
         out_specs=vmem,
         scratch_shapes=[
             pltpu.VMEM((4, 4, width, c1), BF16),
@@ -283,6 +305,11 @@
             pltpu.VMEM(down_proj.shape, BF16),
             pltpu.VMEM(spatial_w.shape, BF16),
             pltpu.VMEM(temporal_w.shape, BF16),
+            pltpu.VMEM(bias_in.shape, F32),
+            pltpu.VMEM(bias_down.shape, F32),
+            pltpu.VMEM(bias_mid.shape, F32),
+            pltpu.VMEM(norm_gain.shape, F32),
+            pltpu.VMEM(latent_proj.shape[::-1], BF16),
             pltpu.VMEM((3, 2, 2, width + 2 * PAD, c1), F32),
             pltpu.VMEM((2, 3, lat, c2), BF16),
             pltpu.VMEM((3, 2, lat + 2 * PAD, c2), F32),
@@ -292,7 +319,7 @@
             pltpu.VMEM((2 * per, 128, c2), BF16),
             pltpu.VMEM((shards, 1, 128), F32),
             pltpu.VMEM((shards, 1, 128), F32),
-            dma((4,)),
+            dma((9,)),
             dma,
             dma((7, 2)),
             dma((5, 2)),

time: 51.9 us -> 45 us (0.87)
  Pallas kernels: 49.9 us -> 43 us
    pallas_call x1, Pallas kernels: 49.9 us -> 43 us  [shards_fn(): pl.pallas_call(functools.partial(kernel, sections, shards), out_shape=jax...]
where the time goes in v2:
time: 45 us; the launch traced here: 44.4 us
  Pallas kernels  43 us (96%)
  local copies, waits for them, and re-layouts  1.42 us (3%)
    pallas_call x1, Pallas kernels, shards_fn(): pl.pallas_call(functools.partial(kernel, sections, shards), out_shape=jax...  43 us
    unnamed x1, local copies, waits for them, and re-layouts  1.42 us

profile of v2, /device:TPU:6, one launch (start us, length us, event | category | flops | bytes accessed | tf_op | source)
XLA Modules:
  0.0 44.4 jit_solution(8312064857209506916)
XLA Ops:
  0.0 43.0 %encoder.1 = f32[96,64]{1,0:T(8,128)} custom-call(bf16[2,2,384,128]{3,2,1,0:T(8,128)(2,1)} %feat.1, bf16[3,3,3,128,128]{4,3,2,1,0:T(8,128)(2,1)} %conv_in.1, f32[128]{0:T(128)} %bias_in_h.1, bf16[2,2,128,256]{3,2,1,0:T(8,128)(2,1)} %down_proj.1, f32[256]{0:T(256)} %bias_down_h.1, bf16[3,3,256,256]{3,2,1,0:T(8,128)(2,1)} %spatial_w.1, ...), custom_call_target="tpu_custom_call" | custom-call | tf_op jit(solution)/shard_map/encoder/pallas_call | solution.py:297
  43.0 1.4 %copy.12 = f32[2,3,16,64]{3,2,1,0:T(8,128)} copy(f32[2,3,16,64]{3,2,1,0:T(8,128)} %bitcast.2) | data formatting | bytes 49152

commit v3 on v2

--- a/solution.py
+++ b/solution.py
@@ -93,13 +93,13 @@
     to_next = [remote(feat.at[f], x.at[f, pl.ds(1, 2)], *pair(2, f), "tm", later) for f in range(2)]
     to_below = [remote(feat.at[f, 1], x.at[2 + f, 0], *pair(0, f), "rows", below) for f in range(2)]
     to_above = [remote(feat.at[f, 0], x.at[2 + f, 3], *pair(1, f), "rows", above) for f in range(2)]
-    relay_below = [remote(x.at[f, 2], x.at[f, 0], *pair(3, f), "rows", below) for f in range(2)]
-    relay_above = [remote(x.at[f, 1], x.at[f, 3], *pair(4, f), "rows", above) for f in range(2)]
+    relay_below = remote(x.at[1, 2], x.at[1, 0], *pair(3, 1), "rows", below)
+    relay_above = remote(x.at[1, 1], x.at[1, 3], *pair(4, 1), "rows", above)
     pass_top = [remote(x.at[2 + f, 0], x.at[f, 0], fs_send.at[5, f], fs_recv.at[3, f], "tm", later) for f in range(2)]
     pass_bottom = [remote(x.at[2 + f, 3], x.at[f, 3], fs_send.at[6, f], fs_recv.at[4, f], "tm", later) for f in range(2)]
 
     for f in range(2):
-        pl.when(has_next)(to_next[f].start)
+        pl.when(has_next)(to_next[1 - f].start)
         pl.when(has_below)(to_below[f].start)
         pl.when(has_above)(to_above[f].start)
 
@@ -141,20 +141,22 @@
 
     both = jnp.logical_and
     relays = both(even, has_prev)
+    passes = (has_next, even)
     for f in range(2):
-        pl.when(has_prev)(to_next[f].wait_recv)
-        pl.when(both(relays, has_below))(relay_below[f].start)
-        pl.when(both(relays, has_above))(relay_above[f].start)
+        pl.when(has_prev)(to_next[1 - f].wait_recv)
+        if f == 0:
+            pl.when(both(relays, has_below))(relay_below.start)
+            pl.when(both(relays, has_above))(relay_above.start)
         pl.when(has_above)(to_below[f].wait_recv)
-        pl.when(both(even, has_above))(pass_top[f].start)
+        pl.when(both(passes[f], has_above))(pass_top[f].start)
         pl.when(has_below)(to_above[f].wait_recv)
-        pl.when(both(even, has_below))(pass_bottom[f].start)
+        pl.when(both(passes[f], has_below))(pass_bottom[f].start)
     hear(1)
+    conv(1, (1,), held, False)
+    conv(1, (2, 3), halo, False)
+    hear(2)
     conv(0, (0, 1), held, False)
     conv(0, (2,), halo, False)
-    hear(2)
-    conv(1, (1,), held, False)
-    conv(1, (2, 3), halo, False)
     for load in loads[4:]:
         load.wait()
     for s in range(2 * per):
@@ -164,11 +166,20 @@
     down_w = w2[...].reshape(4 * w2.shape[2], w2.shape[3])
     act_below = [remote(act.at[f, 1], act.at[f, 0], as_send.at[0, f], as_recv.at[0, f], "rows", below) for f in range(2)]
     act_above = [remote(act.at[f, 1], act.at[f, 2], as_send.at[1, f], as_recv.at[1, f], "rows", above) for f in range(2)]
-    for f in range(2):
-        for n in range(f, 2):
-            if n == 0 or f == 0:
-                pl.when(both(has_prev, has_above))(relay_below[n].wait_recv)
-                pl.when(both(has_prev, has_below))(relay_above[n].wait_recv)
+    loads[2].wait()
+
+    def spatial(f, b, first):
+        weights = jnp.concatenate([w3[b, c] for c in range(3)], axis=-1)
+        total = jnp.dot(act[f, b], weights, preferred_element_type=F32)
+        size = w3.shape[3]
+        for c in range(3):
+            part = total[:, c * size : (c + 1) * size]
+            rows = (c, f, pl.ds(PAD, lat))
+            acc2[rows] = part if first else acc2[rows] + part
+
+    for f in (1, 0):
+        pl.when(both(has_prev, has_above))(pass_top[f].wait_recv)
+        pl.when(both(has_prev, has_below))(pass_bottom[f].wait_recv)
         conv(f, tuple(range(f, 2)), halo, False)
         parts = []
         for o in range(2):
@@ -183,23 +194,12 @@
         act[f, 1] = silu(d.astype(F32)).astype(BF16)
         pl.when(has_below)(act_below[f].start)
         pl.when(has_above)(act_above[f].start)
+        spatial(f, 1, True)
 
     hear(3)
-    loads[2].wait()
     to_later = [remote(sp.at[2 + f], sp.at[f], ss_send.at[f], ss_recv.at[f], "tm", later) for f in range(2)]
 
-    def spatial(f, b, first):
-        weights = jnp.concatenate([w3[b, c] for c in range(3)], axis=-1)
-        total = jnp.dot(act[f, b], weights, preferred_element_type=F32)
-        size = w3.shape[3]
-        for c in range(3):
-            part = total[:, c * size : (c + 1) * size]
-            rows = (c, f, pl.ds(PAD, lat))
-            acc2[rows] = part if first else acc2[rows] + part
-
-    for f in range(2):
-        spatial(f, 1, True)
-    for f in range(2):
+    for f in (1, 0):
         pl.when(has_above)(act_below[f].wait_recv)
         spatial(f, 0, False)
         pl.when(has_below)(act_above[f].wait_recv)
@@ -216,19 +216,16 @@
         return jnp.dot(sp[frame], w4[step], preferred_element_type=F32)
 
     local = [mixed(2, 2), mixed(3, 2) + mixed(2, 1)]
-    for f in range(2):
+    half = normed.shape[3]
+    total = None
+    for f in (1, 0):
         pl.when(has_prev)(to_later[f].wait_recv)
-    half = normed.shape[3]
-    for f in range(2):
         block = down[f].astype(F32) + bias_mid[...][None, :] + local[f]
         block = block + (mixed(0, 0) + mixed(1, 1) if f == 0 else mixed(1, 0))
         scale = lax.rsqrt(jnp.mean(block * block, axis=-1, keepdims=True) + 1e-06)
         value = block * scale * gain[...][None, :]
         for h in range(2):
             normed[f, h] = value[:, h * half : (h + 1) * half]
-
-    total = None
-    for f in range(2):
         for c in range(per):
             rows = jnp.concatenate(
                 [normed[f, h, pl.ds(c, shards, stride=per), :] for h in range(2)], axis=-1
@@ -261,10 +258,10 @@
         for ok, copies in (
             (has_below, (to_below[f], act_below[f])),
             (has_above, (to_above[f], act_above[f])),
-            (both(relays, has_below), (relay_below[f],)),
-            (both(relays, has_above), (relay_above[f],)),
-            (both(even, has_above), (pass_top[f],)),
-            (both(even, has_below), (pass_bottom[f],)),
+            (both(relays, has_below), (relay_below,) * f),
+            (both(relays, has_above), (relay_above,) * f),
+            (both(passes[f], has_above), (pass_top[f],)),
+            (both(passes[f], has_below), (pass_bottom[f],)),
         ):
             for copy in copies:
                 pl.when(ok)(copy.wait_send)

time: 45 us -> 44.4 us (0.987)
  no operation moved by 1% of the time
where the time goes in v3:
time: 44.4 us; the launch traced here: 44.2 us
  Pallas kernels  42.8 us (96%)
  local copies, waits for them, and re-layouts  1.42 us (3%)
    pallas_call x1, Pallas kernels, shards_fn(): pl.pallas_call(functools.partial(kernel, sections, shards), out_shape=jax...  42.8 us
    unnamed x1, local copies, waits for them, and re-layouts  1.42 us

profile of v3, /device:TPU:6, one launch (start us, length us, event | category | flops | bytes accessed | tf_op | source)
XLA Modules:
  0.0 44.2 jit_solution(4797677599592773896)
XLA Ops:
  0.0 42.8 %encoder.1 = f32[96,64]{1,0:T(8,128)} custom-call(bf16[2,2,384,128]{3,2,1,0:T(8,128)(2,1)} %feat.1, bf16[3,3,3,128,128]{4,3,2,1,0:T(8,128)(2,1)} %conv_in.1, f32[128]{0:T(128)} %bias_in_h.1, bf16[2,2,128,256]{3,2,1,0:T(8,128)(2,1)} %down_proj.1, f32[256]{0:T(256)} %bias_down_h.1, bf16[3,3,256,256]{3,2,1,0:T(8,128)(2,1)} %spatial_w.1, ...), custom_call_target="tpu_custom_call" | custom-call | tf_op jit(solution)/shard_map/encoder/pallas_call | solution.py:294
  42.8 1.4 %copy.12 = f32[2,3,16,64]{3,2,1,0:T(8,128)} copy(f32[2,3,16,64]{3,2,1,0:T(8,128)} %bitcast.2) | data formatting | bytes 49152

commit v4 on v3

--- a/solution.py
+++ b/solution.py
@@ -239,7 +239,7 @@
     hear(4)
 
     def token(peer, source):
-        return remote(outbox.at[peer], inbox.at[source], a2a_send.at[peer], a2a_recv.at[source], "rows", peer)
+        return remote(outbox.at[peer], inbox.at[source], a2a_send, a2a_recv, "rows", peer)
 
     middle = shards // 2
     token(lax.rem(row + middle, shards), row).start()
@@ -266,19 +266,10 @@
             for copy in copies:
                 pl.when(ok)(copy.wait_send)
 
-    def land(k, carry):
-        peer = lax.rem(row + k, shards)
-        token(peer, peer).wait_recv()
-        return carry
-
-    def leave(k, carry):
-        peer = lax.rem(row + k, shards)
-        token(peer, peer).wait_send()
-        return carry
-
-    lax.fori_loop(1, shards, land, 0)
+    others = pl.ds(0, shards - 1)
+    pltpu.make_async_copy(outbox.at[others], inbox.at[others], a2a_recv).wait()
     out[...] = jnp.transpose(inbox[:, 0, :])[: 2 * per * chans, :]
-    lax.fori_loop(1, shards, leave, 0)
+    pltpu.make_async_copy(outbox.at[others], inbox.at[others], a2a_send).wait()
 
 
 def shards_fn(
@@ -324,8 +315,8 @@
             dma((2, 2)),
             dma((2,)),
             dma((2,)),
-            dma((shards,)),
-            dma((shards,)),
+            dma,
+            dma,
             pltpu.SemaphoreType.REGULAR((8,)),
         ],
         compiler_params=pltpu.CompilerParams(collective_id=0, has_side_effects=True, vmem_limit_bytes=67_043_328),

time: 44.4 us -> 42.5 us (0.957)
  Pallas kernels: 42.8 us -> 40.9 us
    pallas_call x1, Pallas kernels: 42.8 us -> 40.9 us  [shards_fn(): pl.pallas_call(functools.partial(kernel, sections, shards), out_shape=jax...]
where the time goes in v4:
time: 42.5 us; the launch traced here: 42.3 us
  Pallas kernels  40.9 us (96%)
  local copies, waits for them, and re-layouts  1.42 us (3%)
    pallas_call x1, Pallas kernels, shards_fn(): pl.pallas_call(functools.partial(kernel, sections, shards), out_shape=jax...  40.9 us
    unnamed x1, local copies, waits for them, and re-layouts  1.42 us

profile of v4, /device:TPU:6, one launch (start us, length us, event | category | flops | bytes accessed | tf_op | source)
XLA Modules:
  0.0 42.3 jit_solution(5317954612255309855)
XLA Ops:
  0.0 40.9 %encoder.1 = f32[96,64]{1,0:T(8,128)} custom-call(bf16[2,2,384,128]{3,2,1,0:T(8,128)(2,1)} %feat.1, bf16[3,3,3,128,128]{4,3,2,1,0:T(8,128)(2,1)} %conv_in.1, f32[128]{0:T(128)} %bias_in_h.1, bf16[2,2,128,256]{3,2,1,0:T(8,128)(2,1)} %down_proj.1, f32[256]{0:T(256)} %bias_down_h.1, bf16[3,3,256,256]{3,2,1,0:T(8,128)(2,1)} %spatial_w.1, ...), custom_call_target="tpu_custom_call" | custom-call | tf_op jit(solution)/shard_map/encoder/pallas_call | solution.py:285
  40.9 1.4 %copy.12 = f32[2,3,16,64]{3,2,1,0:T(8,128)} copy(f32[2,3,16,64]{3,2,1,0:T(8,128)} %bitcast.2) | data formatting | bytes 49152

commit v5 on v4

--- a/solution.py
+++ b/solution.py
@@ -42,6 +42,40 @@
     for axis, peer in (("rows", above), ("rows", below), ("tm", later), ("tm", earlier)):
         pl.semaphore_signal(barrier, inc=1, device_id={axis: peer}, device_id_type=MESH)
 
+    pl.semaphore_wait(barrier, 4)
+
+    def pair(slot, frame):
+        return fs_send.at[slot, frame], fs_recv.at[slot, frame]
+
+    to_next = [remote(feat.at[f], x.at[f, pl.ds(1, 2)], *pair(2, f), "tm", later) for f in range(2)]
+    to_below = [remote(feat.at[f, 1], x.at[2 + f, 0], *pair(0, f), "rows", below) for f in range(2)]
+    to_above = [remote(feat.at[f, 0], x.at[2 + f, 3], *pair(1, f), "rows", above) for f in range(2)]
+    relay_below = remote(x.at[1, 2], x.at[1, 0], *pair(3, 1), "rows", below)
+    relay_above = remote(x.at[1, 1], x.at[1, 3], *pair(4, 1), "rows", above)
+    pass_top = [remote(x.at[2 + f, 0], x.at[f, 0], fs_send.at[5, f], fs_recv.at[3, f], "tm", later) for f in range(2)]
+    pass_bottom = [remote(x.at[2 + f, 3], x.at[f, 3], fs_send.at[6, f], fs_recv.at[4, f], "tm", later) for f in range(2)]
+
+    for f in range(2):
+        pl.when(has_next)(to_next[1 - f].start)
+        pl.when(has_below)(to_below[f].start)
+        pl.when(has_above)(to_above[f].start)
+
+    rounds = []
+    while 2 ** len(rounds) <= shards // 4:
+        rounds.append(2 ** len(rounds))
+
+    def tell(step):
+        if step < len(rounds):
+            for peer in (lax.rem(row + rounds[step], shards), lax.rem(row + shards - rounds[step], shards)):
+                pl.semaphore_signal(ready.at[step], inc=1, device_id={"rows": peer}, device_id_type=MESH)
+
+    def hear(step):
+        if step < len(rounds):
+            pl.semaphore_wait(ready.at[step], 2)
+            tell(step + 1)
+
+    tell(0)
+
     own = pltpu.make_async_copy(feat, x.at[pl.ds(2, 2), pl.ds(1, 2)], own_sem)
     own.start()
     loads = [
@@ -84,40 +118,6 @@
             x[f, 3] = jnp.zeros(x.shape[2:], BF16)
         for f in range(2):
             act[f, 2] = jnp.zeros(act.shape[2:], BF16)
-
-    pl.semaphore_wait(barrier, 4)
-
-    def pair(slot, frame):
-        return fs_send.at[slot, frame], fs_recv.at[slot, frame]
-
-    to_next = [remote(feat.at[f], x.at[f, pl.ds(1, 2)], *pair(2, f), "tm", later) for f in range(2)]
-    to_below = [remote(feat.at[f, 1], x.at[2 + f, 0], *pair(0, f), "rows", below) for f in range(2)]
-    to_above = [remote(feat.at[f, 0], x.at[2 + f, 3], *pair(1, f), "rows", above) for f in range(2)]
-    relay_below = remote(x.at[1, 2], x.at[1, 0], *pair(3, 1), "rows", below)
-    relay_above = remote(x.at[1, 1], x.at[1, 3], *pair(4, 1), "rows", above)
-    pass_top = [remote(x.at[2 + f, 0], x.at[f, 0], fs_send.at[5, f], fs_recv.at[3, f], "tm", later) for f in range(2)]
-    pass_bottom = [remote(x.at[2 + f, 3], x.at[f, 3], fs_send.at[6, f], fs_recv.at[4, f], "tm", later) for f in range(2)]
-
-    for f in range(2):
-        pl.when(has_next)(to_next[1 - f].start)
-        pl.when(has_below)(to_below[f].start)
-        pl.when(has_above)(to_above[f].start)
-
-    rounds = []
-    while 2 ** len(rounds) <= shards // 4:
-        rounds.append(2 ** len(rounds))
-
-    def tell(step):
-        if step < len(rounds):
-            for peer in (lax.rem(row + rounds[step], shards), lax.rem(row + shards - rounds[step], shards)):
-                pl.semaphore_signal(ready.at[step], inc=1, device_id={"rows": peer}, device_id_type=MESH)
-
-    def hear(step):
-        if step < len(rounds):
-            pl.semaphore_wait(ready.at[step], 2)
-            tell(step + 1)
-
-    tell(0)
 
     def conv(f, frames, kept, first):
         for o in range(2):

time: 42.5 us -> 42.6 us (level)
  no operation moved by 1% of the time
where the time goes in v5:
time: 42.6 us; the launch traced here: 42.4 us
  Pallas kernels  41 us (96%)
  local copies, waits for them, and re-layouts  1.42 us (3%)
    pallas_call x1, Pallas kernels, shards_fn(): pl.pallas_call(functools.partial(kernel, sections, shards), out_shape=jax...  41 us
    unnamed x1, local copies, waits for them, and re-layouts  1.42 us

profile of v5, /device:TPU:6, one launch (start us, length us, event | category | flops | bytes accessed | tf_op | source)
XLA Modules:
  0.0 42.4 jit_solution(11066441577708306864)
XLA Ops:
  0.0 41.0 %encoder.1 = f32[96,64]{1,0:T(8,128)} custom-call(bf16[2,2,384,128]{3,2,1,0:T(8,128)(2,1)} %feat.1, bf16[3,3,3,128,128]{4,3,2,1,0:T(8,128)(2,1)} %conv_in.1, f32[128]{0:T(128)} %bias_in_h.1, bf16[2,2,128,256]{3,2,1,0:T(8,128)(2,1)} %down_proj.1, f32[256]{0:T(256)} %bias_down_h.1, bf16[3,3,256,256]{3,2,1,0:T(8,128)(2,1)} %spatial_w.1, ...), custom_call_target="tpu_custom_call" | custom-call | tf_op jit(solution)/shard_map/encoder/pallas_call | solution.py:285
  41.0 1.4 %copy.12 = f32[2,3,16,64]{3,2,1,0:T(8,128)} copy(f32[2,3,16,64]{3,2,1,0:T(8,128)} %bitcast.2) | data formatting | bytes 49152

commit v6 on v5

--- a/solution.py
+++ b/solution.py
@@ -154,19 +154,11 @@
     hear(1)
     conv(1, (1,), held, False)
     conv(1, (2, 3), halo, False)
-    hear(2)
-    conv(0, (0, 1), held, False)
-    conv(0, (2,), halo, False)
-    for load in loads[4:]:
-        load.wait()
-    for s in range(2 * per):
-        projs[s, pl.ds(chans * s, chans), :] = proj_t[...]
-
-    loads[1].wait()
+    for i in (1, 4, 5):
+        loads[i].wait()
     down_w = w2[...].reshape(4 * w2.shape[2], w2.shape[3])
     act_below = [remote(act.at[f, 1], act.at[f, 0], as_send.at[0, f], as_recv.at[0, f], "rows", below) for f in range(2)]
     act_above = [remote(act.at[f, 1], act.at[f, 2], as_send.at[1, f], as_recv.at[1, f], "rows", above) for f in range(2)]
-    loads[2].wait()
 
     def spatial(f, b, first):
         weights = jnp.concatenate([w3[b, c] for c in range(3)], axis=-1)
@@ -178,9 +170,11 @@
             acc2[rows] = part if first else acc2[rows] + part
 
     for f in (1, 0):
+        if f == 0:
+            conv(0, (0, 1), held, False)
         pl.when(both(has_prev, has_above))(pass_top[f].wait_recv)
         pl.when(both(has_prev, has_below))(pass_bottom[f].wait_recv)
-        conv(f, tuple(range(f, 2)), halo, False)
+        conv(f, (1,) if f == 1 else (0, 1, 2), halo, False)
         parts = []
         for o in range(2):
             for b in range(2):
@@ -194,9 +188,17 @@
         act[f, 1] = silu(d.astype(F32)).astype(BF16)
         pl.when(has_below)(act_below[f].start)
         pl.when(has_above)(act_above[f].start)
-        spatial(f, 1, True)
-
+        if f == 1:
+            hear(2)
+            loads[2].wait()
+            spatial(1, 1, True)
+
+    spatial(0, 1, True)
     hear(3)
+    for i in (6, 7, 8):
+        loads[i].wait()
+    for s in range(2 * per):
+        projs[s, pl.ds(chans * s, chans), :] = proj_t[...]
     to_later = [remote(sp.at[2 + f], sp.at[f], ss_send.at[f], ss_recv.at[f], "tm", later) for f in range(2)]
 
     for f in (1, 0):
@@ -221,9 +223,10 @@
     for f in (1, 0):
         pl.when(has_prev)(to_later[f].wait_recv)
         block = down[f].astype(F32) + bias_mid[...][None, :] + local[f]
-        block = block + (mixed(0, 0) + mixed(1, 1) if f == 0 else mixed(1, 0))
+        block = block + (mixed(0, 0) + early if f == 0 else mixed(1, 0))
         scale = lax.rsqrt(jnp.mean(block * block, axis=-1, keepdims=True) + 1e-06)
         value = block * scale * gain[...][None, :]
+        early = mixed(1, 1) if f == 1 else None
         for h in range(2):
             normed[f, h] = value[:, h * half : (h + 1) * half]
         for c in range(per):

time: 42.6 us -> 42.8 us (level)
  no operation moved by 1% of the time
where the time goes in v6:
time: 42.8 us; the launch traced here: 42.2 us
  Pallas kernels  40.8 us (95%)
  local copies, waits for them, and re-layouts  1.42 us (3%)
    pallas_call x1, Pallas kernels, shards_fn(): pl.pallas_call(functools.partial(kernel, sections, shards), out_shape=jax...  40.8 us
    unnamed x1, local copies, waits for them, and re-layouts  1.42 us

profile of v6, /device:TPU:6, one launch (start us, length us, event | category | flops | bytes accessed | tf_op | source)
XLA Modules:
  0.0 42.2 jit_solution(18180180830213013305)
XLA Ops:
  0.0 40.8 %encoder.1 = f32[96,64]{1,0:T(8,128)} custom-call(bf16[2,2,384,128]{3,2,1,0:T(8,128)(2,1)} %feat.1, bf16[3,3,3,128,128]{4,3,2,1,0:T(8,128)(2,1)} %conv_in.1, f32[128]{0:T(128)} %bias_in_h.1, bf16[2,2,128,256]{3,2,1,0:T(8,128)(2,1)} %down_proj.1, f32[256]{0:T(256)} %bias_down_h.1, bf16[3,3,256,256]{3,2,1,0:T(8,128)(2,1)} %spatial_w.1, ...), custom_call_target="tpu_custom_call" | custom-call | tf_op jit(solution)/shard_map/encoder/pallas_call | solution.py:288
  40.8 1.4 %copy.12 = f32[2,3,16,64]{3,2,1,0:T(8,128)} copy(f32[2,3,16,64]{3,2,1,0:T(8,128)} %bitcast.2) | data formatting | bytes 49152

commit v7 on v5

--- a/solution.py
+++ b/solution.py
@@ -268,7 +268,7 @@
 
     others = pl.ds(0, shards - 1)
     pltpu.make_async_copy(outbox.at[others], inbox.at[others], a2a_recv).wait()
-    out[...] = jnp.transpose(inbox[:, 0, :])[: 2 * per * chans, :]
+    out[...] = inbox[:, 0, :]
     pltpu.make_async_copy(outbox.at[others], inbox.at[others], a2a_send).wait()
 
 
@@ -284,7 +284,7 @@
     dma = pltpu.SemaphoreType.DMA
     tokens = pl.pallas_call(
         functools.partial(kernel, sections, shards),
-        out_shape=jax.ShapeDtypeStruct((frames * per * chans, shards), F32),
+        out_shape=jax.ShapeDtypeStruct((shards, 128), F32),
         in_specs=[hbm] * 10,
         out_specs=vmem,
         scratch_shapes=[
@@ -322,7 +322,7 @@
         compiler_params=pltpu.CompilerParams(collective_id=0, has_side_effects=True, vmem_limit_bytes=67_043_328),
         name="encoder",
     )(features, conv_in, bias_in, down_proj, bias_down, spatial_w, temporal_w, bias_mid, norm_gain, latent_proj.T)
-    return tokens.reshape(frames, per, chans, shards)
+    return tokens[:, : frames * per * chans].T.reshape(frames, per, chans, shards)
 
 
 def solution(mesh):

time: 42.6 us -> 42.6 us (level)
    transpose x0 -> x2, local copies, waits for them, and re-layouts: none -> 1.47 us  [shards_fn(): tokens[:, :frames * per * chans].T.reshape(frames, per, chans, shards)]
    unnamed x1 -> x0, local copies, waits for them, and re-layouts: 1.42 us -> none
where the time goes in v7:
time: 42.6 us; the launch traced here: 42.3 us
  Pallas kernels  40.9 us (96%)
  local copies, waits for them, and re-layouts  1.47 us (3%)
    pallas_call x1, Pallas kernels, shards_fn(): pl.pallas_call(functools.partial(kernel, sections, shards), out_shape=jax...  40.9 us
    transpose x2, local copies, waits for them, and re-layouts, shards_fn(): tokens[:, :frames * per * chans].T.reshape(frames, per, chans, shards)  1.47 us

profile of v7, /device:TPU:6, one launch (start us, length us, event | category | flops | bytes accessed | tf_op | source)
XLA Modules:
  0.0 42.3 jit_solution(5165251170958146978)
XLA Ops:
  0.0 40.9 %encoder.1 = f32[64,128]{1,0:T(8,128)} custom-call(bf16[2,2,384,128]{3,2,1,0:T(8,128)(2,1)} %feat.1, bf16[3,3,3,128,128]{4,3,2,1,0:T(8,128)(2,1)} %conv_in.1, f32[128]{0:T(128)} %bias_in_h.1, bf16[2,2,128,256]{3,2,1,0:T(8,128)(2,1)} %down_proj.1, f32[256]{0:T(256)} %bias_down_h.1, bf16[3,3,256,256]{3,2,1,0:T(8,128)(2,1)} %spatial_w.1, ...), custom_call_target="tpu_custom_call" | custom-call | tf_op jit(solution)/shard_map/encoder/pallas_call | solution.py:285
  40.9 0.8 %slice_bitcast_fusion = f32[96,64]{0,1:T(8,128)S(1)} fusion(f32[64,128]{1,0:T(8,128)} %encoder.1), kind=kLoop, calls=%fused_computation | loop fusion | bytes 49152 | tf_op jit(solution)/shard_map/transpose | solution.py:325
  41.6 0.7 %copy.12 = f32[96,64]{1,0:T(8,128)} copy(f32[96,64]{0,1:T(8,128)S(1)} %slice_bitcast_fusion) | data formatting | bytes 49152 | tf_op jit(solution)/shard_map/transpose | solution.py:325
